TPU v7x, 128 devices: a whole 4x4x4 slice. The times are simulated.
128 devices in a mesh: scen: 4 (over x), path: 32 (over z, y, core).
Axes of the slice: x: 4, y: 4, z: 4, core: 2. Of those that a mesh axis runs over, the one named last changes fastest.
Arguments:
- states: float32 [4, 36, 8, 16384], P('scen', None, None, 'path'), may hold values from -1.5 to 1.5
- exercise_dates: int32 [4, 2], P('scen'), may hold values from 0 to 35, as said below
- itm_mask: int32 [4, 2, 16384], P('scen', None, 'path'), may hold values 0 or 1
- surrender: float32 [4, 36, 16384], P('scen', None, 'path'), may hold values from -0.5 to 1
- terminal: float32 [4, 16384], P('scen', 'path'), may hold values from -5 to 5
- discount: float32 [4, 2], P('scen'), may hold values from 0.5 to 1
- ls_table: int32 [256, 8], replicated, may hold values from 0 to 2, as said below
- proxy_table: int32 [2048, 8], replicated, may hold values from 0 to 2, as said below
Outputs:
- path_values: float32 [4, 16384], P('scen', 'path')
- coefficients: float32 [4, 2, 256], P('scen')
- proxy_gram: float32 [2048, 2048], P(('scen', 'path'))
- proxy_rhs: float32 [2048], P(('scen', 'path'))
Inputs may be any that keep to these rules, and one draw needn't show every extreme that they name: `exercise_dates`: the first exercise date lies below 18 and the second at or above it. `ls_table`: no two rows are equal. `proxy_table`: no two rows are equal.
All inputs are finite; a program needn't handle non-finite values. No bound on the sum of `itm_mask` on one device may be relied on, other than what follows from the above.
Results may differ from a plain program's by a relative error of at most 0.005.
Values sent between devices are 32-bit elements; how exact they have to be, the bound alone decides.
A program may use at most 64 MiB of HBM per device.

v0:
```python
import functools

import jax
import jax.numpy as jnp
from jax import lax
from jax.experimental import pallas as pl
from jax.experimental.pallas import tpu as pltpu
from jax.sharding import PartitionSpec as P

MESH = pl.DeviceIdType.MESH
HI = lax.Precision.HIGHEST
F32, BF16 = jnp.float32, jnp.bfloat16
ROOT_HALF = 0.7071067811865476
SIDE = 640
CHUNK = 400
PAIRS = 96
STEP = 32


def nt(a, b):
    return lax.dot_general(a, b, (((1,), (1,)), ((), ())), preferred_element_type=F32)


def nn(a, b):
    return jnp.dot(a, b, preferred_element_type=F32)


def halves(x):
    high = x.astype(BF16)
    return high, (x - high.astype(F32)).astype(BF16)


def three_rows(x):
    high = x.astype(BF16).astype(F32)
    rest = x - high
    mid = rest.astype(BF16).astype(F32)
    sub = lax.broadcasted_iota(jnp.int32, (8, x.shape[1]), 0)
    low = rest - mid
    return jnp.where(
        sub == 0, high, jnp.where(sub == 1, mid, jnp.where(sub == 2, low, 0.0))
    ).astype(BF16)


def add_rows(x):
    return x[0:1] + x[1:2] + x[2:3]


def products(factors, pair_a, pair_b, out, levels):
    count = levels * levels
    for i in range(levels):
        for j in range(levels):
            row = i * levels + j
            pair_a[row : row + 1, :] = factors[0][i] * factors[1][j]
            pair_b[row : row + 1, :] = factors[2][i] * factors[3][j]
    for i in range(count):
        out[i * count : (i + 1) * count, :] = pair_a[i : i + 1, :] * pair_b[0:count, :]


def sweep_small(e, n):
    def at(i, j):
        return e[min(i, j), max(i, j)]

    for k in range(0, n, 2):
        p, q, s = e[k, k], e[k, k + 1], e[k + 1, k + 1]
        w = 1.0 / (p * s - q * q)
        pw, qw, sw = p * w, q * w, s * w
        others = [i for i in range(n) if i not in (k, k + 1)]
        r0 = {i: at(k, i) for i in others}
        r1 = {i: at(k + 1, i) for i in others}
        x0 = {i: sw * r0[i] - qw * r1[i] for i in others}
        x1 = {i: pw * r1[i] - qw * r0[i] for i in others}
        for i in others:
            for j in others:
                if i <= j:
                    e[i, j] = e[i, j] - (r0[i] * x0[j] + r1[i] * x1[j])
        for i in others:
            e[min(i, k), max(i, k)] = x0[i]
            e[min(i, k + 1), max(i, k + 1)] = x1[i]
        e[k, k], e[k, k + 1], e[k + 1, k + 1] = -sw, qw, -pw
    return e


def tree_sum(terms):
    while len(terms) > 1:
        terms = [terms[t] + terms[t + 1] for t in range(0, len(terms), 2)]
    return terms[0]


def leaf(a, e_ref, r_ref):
    lane = lax.broadcasted_iota(jnp.int32, (STEP, 128), 1)
    lane8 = lax.broadcasted_iota(jnp.int32, (8, 128), 1)
    sub8 = lax.broadcasted_iota(jnp.int32, (8, 128), 0)
    half = lane - lane % 64
    in_half = lane8 % 64
    for o in range(0, STEP, 8):
        cols = [jnp.take_along_axis(a, half + (o + j), axis=1) for j in range(8)]
        r_ref[...] = a[o : o + 8, :]
        for j in range(8):
            e_ref[j] = cols[j][o : o + 8, :]
        e = {(i, j): e_ref[j, pl.ds(i, 8, stride=0), :] for i in range(8) for j in range(i, 8)}
        e = sweep_small(e, 8)
        rows = [r_ref[pl.ds(i, 8, stride=0), :] for i in range(8)]
        xs = []
        for i in range(8):
            entries = [e[min(i, j), max(i, j)] for j in range(8)]
            x = -tree_sum([entries[j] * rows[j] for j in range(8)])
            for j in range(8):
                x = jnp.where(in_half == o + j, entries[j], x)
            xs.append(x)
        tile = xs[0]
        for i in range(1, 8):
            tile = jnp.where(sub8 == i, xs[i], tile)
        inside = (in_half >= o) & (in_half < o + 8)
        tiles = []
        for t in range(0, STEP, 8):
            if t == o:
                tiles.append(tile)
            else:
                base = jnp.where(inside, 0.0, a[t : t + 8, :])
                tiles.append(base - tree_sum([cols[j][t : t + 8, :] * xs[j] for j in range(8)]))
        a = jnp.concatenate(tiles, axis=0)
    return a


def eliminate(a_ref, e_ref, r_ref, start, stop):
    n = a_ref.shape[1]
    lane = lax.broadcasted_iota(jnp.int32, (STEP, n), 1)
    lane1 = lax.broadcasted_iota(jnp.int32, (STEP, 128), 1)
    lane2 = lax.broadcasted_iota(jnp.int32, (n - STEP, n), 1)

    def body(k, _):
        first = [a_ref[d, 0:STEP, 0:128] for d in range(2)]
        both = leaf(jnp.where(lane1 < 64, first[0], pltpu.roll(first[1], 64, 1)), e_ref, r_ref)
        for d, neg in enumerate((both, pltpu.roll(both, 64, 1))):
            r = a_ref[d, 0:STEP, :]
            rest = a_ref[d, STEP:, :]
            x = jnp.dot(neg[:, 0:STEP], r, precision=HI, preferred_element_type=F32)
            xt = jnp.where(lane < STEP, jnp.concatenate([neg, neg], axis=1), -x)
            new = jnp.where(lane2 < STEP, 0.0, rest) - jnp.dot(
                rest[:, 0:STEP], xt, precision=HI, preferred_element_type=F32
            )
            a_ref[d, 0 : n - STEP, :] = pltpu.roll(new, n - STEP, 1)
            a_ref[d, n - STEP :, :] = pltpu.roll(xt, n - STEP, 1)
        return 0

    lax.fori_loop(start, stop, body, 0)


def arrived(buffer, sem):
    pltpu.make_async_copy(buffer, buffer, sem).wait()


def step_kernel(
    path_devices, scens,
    dates, disc, table_any, states, mask, surrender, terminal, ls_columns, table,
    values_out, coef_out, gram_out, rhs_out,
    pair_a, pair_b, left, right, whole, design, gram, gram_half, gram_acc, gram_in, gram_all,
    rhs_own, rhs_in, rhs0_own, rhs0_in, a_ref, e_ref, r_ref,
    mom, mom_half, mom_acc, x_in, x_sum, seat_out, seat_in, seat_all, full, ls_table, mine, pattern, pick_l, pick_r, y_high, y_low, z_pack,
    low, high, left3, right3, parts, parts_in, mine_part, mine_in,
    gh_s, gh_r, g_s, g_r, ga_s, ga_r, gf_s, gf_r, rhs_s, rhs_r, rhs0_s, rhs0_r,
    half_s, half_r, xr_s, xr_r, sr_s, sr_r, sa_s, sa_r, xa_s, xa_r, fw_s, fw_r, pa_s, pa_r, pb_s, pb_r, own_s,
):
    paths = terminal.shape[1]
    terms = ls_columns.shape[1]
    s, p = lax.axis_index("scen"), lax.axis_index("path")
    core, seat = p % 2, p // 2
    seats = path_devices // 2
    rows = gram_out.shape[0]
    index = s * path_devices + p
    first_own = rows * (index % (128 // rows))
    total_paths = paths * path_devices
    scale = 1.0 / total_paths
    own_scale = 1.0 / (total_paths * scens)
    partner = (s, seat * 2 + 1 - core)

    def path_peer(d):
        return (p + d) % path_devices

    def seat_peer(d):
        return (seat + d) % seats

    def scen_peer(d):
        return (s + d) % scens

    def seat_id(j):
        return (s, j * 2 + core)

    def send(src, dst, send_sem, recv_sem, target):
        return pltpu.make_async_remote_copy(
            src_ref=src, dst_ref=dst, send_sem=send_sem, recv_sem=recv_sem,
            device_id=target, device_id_type=MESH)

    def gram_half_copy():
        return send(gram.at[1 - core], gram_half, gh_s, gh_r, partner)

    def gram_copy(j):
        return send(gram_acc.at[j], gram_in.at[seat], g_s.at[j], g_r.at[seat], seat_id(j))

    def gram_all_copy(j):
        block = gram_all.at[core, seat]
        return send(block, block, ga_s.at[j], ga_r.at[seat], seat_id(j))

    def gram_forward(j):
        block = gram_all.at[core, j]
        return send(block, block, gf_s.at[j], gf_r.at[j], partner)

    def rhs_copy(q):
        return send(rhs_own, rhs_in.at[p], rhs_s.at[q], rhs_r.at[p], (s, q))

    def rhs0_copy(q):
        return send(rhs0_own, rhs0_in.at[p], rhs0_s.at[q], rhs0_r.at[p], (s, q))

    def half_copy():
        return send(mom.at[1 - core], mom_half, half_s, half_r, partner)

    def x_copy(t):
        return send(mom_acc.at[t], x_in.at[s], xr_s.at[t], xr_r.at[s], (t, p))

    def seat_copy(j):
        return send(seat_out.at[j], seat_in.at[seat], sr_s.at[j], sr_r.at[seat], seat_id(j))

    def seat_all_copy(j):
        block = seat_all.at[seat]
        return send(block, block, sa_s.at[j], sa_r.at[seat], seat_id(j))

    def full_copy(t):
        block = full.at[core, s]
        return send(block, block, xa_s.at[t], xa_r.at[s], (t, p))

    def forward_copy(t):
        block = full.at[core, t]
        return send(block, block, fw_s.at[t], fw_r.at[t], partner)

    def part_copy(q):
        return send(parts.at[:, q // 8], parts_in.at[p], pa_s.at[q], pa_r.at[p], (s, q))

    def mine_copy(t):
        return send(mine_part.at[t], mine_in.at[s], pb_s.at[t], pb_r.at[s], (t, p))

    barrier = pltpu.get_barrier_semaphore()

    @pl.loop(1, path_devices)
    def _(d):
        pl.semaphore_signal(barrier, inc=1, device_id=(s, path_peer(d)), device_id_type=MESH)

    @pl.loop(1, scens)
    def _(d):
        pl.semaphore_signal(barrier, inc=1, device_id=(scen_peer(d), p), device_id_type=MESH)

    own_tile = pltpu.make_async_copy(
        table_any.at[:, pl.ds(pl.multiple_of(128 * (index // (128 // rows)), 128), 128)], mine, own_s
    )
    own_tile.start()
    ls_table[...] = ls_columns[...].T

    early = states[dates[0]]
    for backward in (1, 0):
        u = early if backward == 0 else states[dates[1]]
        h = (u * u - 1.0) * ROOT_HALF
        for top in range(0, terms, 32):
            t = ls_table[top : top + 32, :]
            result = None
            for v in range(8):
                degree = jnp.broadcast_to(t[:, v : v + 1], (32, paths))
                level = jnp.where(
                    degree == 1, u[v : v + 1, :], jnp.where(degree == 2, h[v : v + 1, :], 1.0)
                )
                result = level if result is None else result * level
            design[backward, top : top + 32, :] = result.astype(BF16)
        live = design[backward]
        weighted = live * mask[backward : backward + 1, :].astype(F32).astype(BF16)
        g = nt(weighted, live)
        blocks = jnp.concatenate([g[0:128, 0:128], g[128:256, 0:128], g[128:256, 128:256]], axis=0)
        gram[backward] = blocks.reshape(gram.shape[1:])
        if backward == 1:
            rhs_own[...] = add_rows(nt(three_rows(disc[1] * terminal[...]), weighted))

    pl.semaphore_wait(barrier, path_devices - 1 + scens - 1)
    gram_half_copy().start()

    g = early * early - 1.0
    h = g * ROOT_HALF
    one = jnp.ones((1, paths), F32)

    def five(v):
        x, y = early[v : v + 1, :], g[v : v + 1, :]
        return [one, x, y, x * y, y * y]

    for side, first in ((left, 0), (right, 4)):
        side[624:SIDE, :] = jnp.zeros((SIDE - 624, paths), F32)
        products([five(first + v) for v in range(4)], pair_a, pair_b, side, 5)

    gram_half_copy().wait()
    gram_acc[...] = gram[core] + gram_half[...]

    @pl.loop(1, seats)
    def _(d):
        gram_copy(seat_peer(d)).start()

    lh, ll = halves(left[...])
    rh, rl = halves(right[...])
    moments = nt(lh, rh) + nt(lh, rl) + nt(ll, rh)
    for k in range(SIDE // 128):
        low_row = k * SIDE
        while low_row < (k + 1) * SIDE:
            c = low_row // CHUNK
            top_row = min((k + 1) * SIDE, (c + 1) * CHUNK)
            mom[c // scens, c % scens, low_row - c * CHUNK : top_row - c * CHUNK, :] = moments[
                low_row - k * SIDE : top_row - k * SIDE, k * 128 : (k + 1) * 128
            ]
            low_row = top_row
    half_copy().start()

    @pl.loop(1, path_devices)
    def _(d):
        rhs_copy(path_peer(d)).start()

    @pl.loop(1, seats)
    def _(d):
        arrived(gram_in.at[seat_peer(d)], g_r.at[seat_peer(d)])

    def add_gram(d, carry):
        return carry + gram_in[seat_peer(d)]

    gram_all[core, seat] = lax.fori_loop(1, seats, add_gram, gram_acc[seat])

    @pl.loop(1, seats)
    def _(d):
        gram_all_copy(seat_peer(d)).start()

    gram_forward(seat).start()

    half_copy().wait()
    for t in range(scens):
        mom_acc[t] = mom[core, t] + mom_half[t]

    @pl.loop(1, scens)
    def _(d):
        x_copy(scen_peer(d)).start()

    row = lax.broadcasted_iota(jnp.int32, high.shape, 0)
    for first, is_low in ((0, True), (4, False)):
        t = [table[first + v : first + v + 1, :] for v in range(4)]
        code = ((t[0] * 3 + t[1]) * 3 + t[2]) * 3 + t[3]
        hot = jnp.where(row == code, 1.0, 0.0)
        if is_low:
            low[0:PAIRS, :] = hot.astype(BF16)
            low[PAIRS:128, :] = jnp.zeros((128 - PAIRS, hot.shape[1]), BF16)
            low[128 : 128 + PAIRS, :] = hot.astype(BF16)
            low[128 + PAIRS : 256, :] = jnp.zeros((128 - PAIRS, hot.shape[1]), BF16)
        else:
            high[...] = hot

    @pl.loop(1, seats)
    def _(d):
        j = seat_peer(d)
        arrived(gram_all.at[core, j], ga_r.at[j])
        gram_forward(j).start()

    @pl.loop(1, scens)
    def _(d):
        arrived(x_in.at[scen_peer(d)], xr_r.at[scen_peer(d)])

    x_sum[...] = lax.fori_loop(1, scens, lambda d, carry: carry + x_in[scen_peer(d)], mom_acc[s])
    own_part = CHUNK // seats
    for j in range(seats):
        seat_out[j] = x_sum[j * own_part : (j + 1) * own_part, :]

    @pl.loop(1, seats)
    def _(d):
        seat_copy(seat_peer(d)).start()

    @pl.loop(0, seats)
    def _(j):
        arrived(gram_all.at[1 - core, j], gf_r.at[j])

    ri = lax.broadcasted_iota(jnp.int32, (128, 128), 0)
    ci = lax.broadcasted_iota(jnp.int32, (128, 128), 1)
    ridge = jnp.where(ri == ci, 0.05, 0.0)
    for d in range(2):
        stack = gram_all[d].reshape(384, 128) * scale
        corner = stack[128:256, :]
        a_ref[d, 0:128, 0:128] = stack[0:128, :] + ridge
        a_ref[d, 128:256, 0:128] = corner
        a_ref[d, 0:128, 128:256] = corner.T
        a_ref[d, 128:256, 128:256] = stack[256:384, :] + ridge
    steps = terms // STEP
    eliminate(a_ref, e_ref, r_ref, 0, steps // 4)

    @pl.loop(1, seats)
    def _(d):
        arrived(seat_in.at[seat_peer(d)], sr_r.at[seat_peer(d)])

    seat_all[seat] = lax.fori_loop(
        1, seats, lambda d, carry: carry + seat_in[seat_peer(d)], seat_out[seat]
    )

    @pl.loop(1, seats)
    def _(d):
        seat_all_copy(seat_peer(d)).start()

    eliminate(a_ref, e_ref, r_ref, steps // 4, steps // 2)

    @pl.loop(1, seats)
    def _(d):
        arrived(seat_all.at[seat_peer(d)], sa_r.at[seat_peer(d)])

    for j in range(seats):
        full[core, s, j * own_part : (j + 1) * own_part, :] = seat_all[j]

    @pl.loop(1, scens)
    def _(d):
        full_copy(scen_peer(d)).start()

    forward_copy(s).start()
    eliminate(a_ref, e_ref, r_ref, steps // 2, steps)

    @pl.loop(1, path_devices)
    def _(d):
        arrived(rhs_in.at[path_peer(d)], rhs_r.at[path_peer(d)])

    def add_rhs(d, carry):
        return carry + rhs_in[path_peer(d)]

    rhs = lax.fori_loop(1, path_devices, add_rhs, rhs_own[...]) * scale
    coef = -jnp.dot(
        jnp.broadcast_to(rhs, (8, terms)), a_ref[1], precision=HI, preferred_element_type=F32
    )[0:1]
    coef_out[1:2, :] = coef
    continuation = add_rows(nn(three_rows(coef), design[1]))
    payoff = surrender[dates[1]]
    values = disc[1] * terminal[...]
    values = jnp.where(mask[1:2, :] > 0, jnp.maximum(payoff, continuation), values)
    values = disc[0] * values
    weighted = design[0] * mask[0:1, :].astype(F32).astype(BF16)
    rhs0_own[...] = add_rows(nt(three_rows(values), weighted))

    @pl.loop(1, path_devices)
    def _(d):
        rhs0_copy(path_peer(d)).start()

    for out, first in ((left3, 0), (right3, 4)):
        out[80:PAIRS, :] = jnp.zeros((PAIRS - 80, paths), F32)
        levels = [
            [one, early[first + v : first + v + 1, :], h[first + v : first + v + 1, :]]
            for v in range(4)
        ]
        products(levels, pair_a, pair_b, out, 3)
    prow = lax.broadcasted_iota(jnp.int32, (PAIRS, 1), 0)
    plane = lax.broadcasted_iota(jnp.int32, (1, SIDE), 1)
    for v, (three, five_) in enumerate(((27, 125), (9, 25), (3, 5), (1, 1))):
        b = jnp.where(prow < 81, (prow // three) % 3, -9)
        m = jnp.where(plane < 625, (plane // five_) % 5, -20)
        b, m = jnp.broadcast_to(b, (PAIRS, SIDE)), jnp.broadcast_to(m, (PAIRS, SIDE))
        ones = ((b == 0) & (m == 1)) | ((b == 1) & ((m == 0) | (m == 2))) | ((b == 2) & (m == 3))
        pattern[v, 0] = jnp.where(m == b, 1.0, 0.0).astype(BF16)
        pattern[v, 1] = jnp.where(ones, 1.0, 0.0).astype(BF16)
        pattern[v, 2] = jnp.where(m == b + 2, 1.0, 0.0).astype(BF16)

    @pl.loop(1, scens)
    def _(d):
        t = scen_peer(d)
        arrived(full.at[core, t], xa_r.at[t])
        forward_copy(t).start()

    @pl.loop(1, path_devices)
    def _(d):
        arrived(rhs0_in.at[path_peer(d)], rhs0_r.at[path_peer(d)])

    def add_rhs0(d, carry):
        return carry + rhs0_in[path_peer(d)]

    rhs = lax.fori_loop(1, path_devices, add_rhs0, rhs0_own[...]) * scale
    coef = -jnp.dot(
        jnp.broadcast_to(rhs, (8, terms)), a_ref[0], precision=HI, preferred_element_type=F32
    )[0:1]
    coef_out[0:1, :] = coef
    continuation = add_rows(nn(three_rows(coef), design[0]))
    payoff = surrender[dates[0]]
    final = jnp.where(mask[0:1, :] > 0, jnp.maximum(payoff, continuation), values)
    values_out[...] = final

    rounded = final.astype(BF16).astype(F32)
    lh, ll = halves(left3[...] * rounded)
    rh, rl = halves(right3[...])
    wh, wl = halves(nt(rh, lh) + nt(rh, ll) + nt(rl, lh))
    hot = low[0:PAIRS, :]
    picked = jnp.sum((nn(wh, hot) + nn(wl, hot)) * high[...], axis=0, keepdims=True)
    for t in range(parts.shape[0]):
        for q in range(parts.shape[1]):
            k = (t * parts.shape[1] + q) * 128
            parts[t, q] = picked[:, k : k + 128]

    @pl.loop(1, path_devices)
    def _(d):
        part_copy(path_peer(d)).start()

    own_tile.wait()

    @pl.loop(0, rows)
    def _(r):
        def pattern_of(first):
            result = None
            for v in range(4):
                block = pattern[v, mine[first + v, first_own + r]]
                result = block if result is None else result * block
            return result

        pick_l[r] = pattern_of(0)
        pick_r[r] = pattern_of(4)

    @pl.loop(0, scens)
    def _(t):
        arrived(full.at[1 - core, t], fw_r.at[t])

    for k in range(SIDE // 128):
        low_row = k * SIDE
        while low_row < (k + 1) * SIDE:
            c = low_row // CHUNK
            top_row = min((k + 1) * SIDE, (c + 1) * CHUNK)
            whole[low_row - k * SIDE : top_row - k * SIDE, k * 128 : (k + 1) * 128] = full[
                c // scens, c % scens, low_row - c * CHUNK : top_row - c * CHUNK, :
            ]
            low_row = top_row
    mh, ml = halves(whole[...])
    picks = pick_l[...].reshape(rows * PAIRS, SIDE)
    yh, yl = halves(nn(picks, mh) + nn(picks, ml))
    y_high[...] = yh.reshape(y_high.shape)
    y_low[...] = yl.reshape(y_low.shape)

    @pl.loop(1, path_devices)
    def _(d):
        arrived(parts_in.at[path_peer(d)], pa_r.at[path_peer(d)])

    def add_part(d, carry):
        return carry + parts_in[path_peer(d)]

    mine_part[...] = lax.fori_loop(1, path_devices, add_part, parts[:, p // 8])

    @pl.loop(1, scens)
    def _(d):
        mine_copy(scen_peer(d)).start()

    z_pack[...] = jnp.zeros(z_pack.shape, BF16)

    @pl.loop(0, rows)
    def _(r):
        zh, zl = halves(nt(pick_r[r], y_high[r]) + nt(pick_r[r], y_low[r]))
        z_pack[r, :, 0:PAIRS] = zh
        z_pack[r, :, 128 : 128 + PAIRS] = zl

    @pl.loop(1, scens)
    def _(d):
        arrived(mine_in.at[scen_peer(d)], pb_r.at[scen_peer(d)])

    def add_mine(d, carry):
        return carry + mine_in[scen_peer(d)]

    last = lax.fori_loop(1, scens, add_mine, mine_part[s])
    last = pltpu.roll(jnp.broadcast_to(last, (8, 128)), (128 - rows * (p % 8)) % 128, 1)
    rhs_out[...] = last[0:1] * own_scale

    column = None
    for v in range(8):
        factor = jnp.where(table[v : v + 1, :] == 2, ROOT_HALF, 1.0)
        column = factor if column is None else column * factor

    @pl.loop(0, rows // 8)
    def _(block):
        lines = []
        for k in range(8):
            r = block * 8 + k
            own = own_scale
            for v in range(8):
                own = own * jnp.where(mine[v, first_own + r] == 2, ROOT_HALF, 1.0)
            picked = nn(z_pack[r], low[...]) * high[...]
            lines.append(jnp.sum(picked, axis=0, keepdims=True) * (column * own))
        gram_out[pl.ds(pl.multiple_of(block * 8, 8), 8), :] = jnp.concatenate(lines, axis=0)

    gram_forward(seat).wait_send()

    @pl.loop(1, seats)
    def _(d):
        j = seat_peer(d)
        gram_copy(j).wait_send()
        gram_all_copy(j).wait_send()
        gram_forward(j).wait_send()

    @pl.loop(1, path_devices)
    def _(d):
        q = path_peer(d)
        rhs_copy(q).wait_send()
        rhs0_copy(q).wait_send()
        part_copy(q).wait_send()

    @pl.loop(1, seats)
    def _(d):
        j = seat_peer(d)
        seat_copy(j).wait_send()
        seat_all_copy(j).wait_send()

    @pl.loop(1, scens)
    def _(d):
        t = scen_peer(d)
        x_copy(t).wait_send()
        full_copy(t).wait_send()
        mine_copy(t).wait_send()

    @pl.loop(0, scens)
    def _(t):
        forward_copy(t).wait_send()


VMEM = pl.BlockSpec(memory_space=pltpu.VMEM)
SMEM = pl.BlockSpec(memory_space=pltpu.SMEM)
DMA = pltpu.SemaphoreType.DMA


def on_device(
    states, exercise_dates, itm_mask, surrender, terminal, discount, ls_table, proxy_table
):
    scens, path_devices = lax.axis_size("scen"), lax.axis_size("path")
    paths = states.shape[3]
    terms, proxy_terms = ls_table.shape[0], proxy_table.shape[0]
    devices = scens * path_devices
    seats = path_devices // 2
    own_rows = proxy_terms // devices
    columns = proxy_table.T
    rows = 384 // seats
    buffer = pltpu.VMEM
    tiles = proxy_terms // 128

    values, coefficients, proxy_gram, proxy_rhs = pl.pallas_call(
        functools.partial(step_kernel, path_devices, scens),
        out_shape=(
            jax.ShapeDtypeStruct((1, paths), F32),
            jax.ShapeDtypeStruct((2, terms), F32),
            jax.ShapeDtypeStruct((own_rows, proxy_terms), F32),
            jax.ShapeDtypeStruct((1, 128), F32),
        ),
        in_specs=[SMEM] * 2 + [pl.BlockSpec(memory_space=pl.ANY)] + [VMEM] * 6,
        out_specs=[VMEM] * 4,
        scratch_shapes=[
            buffer((32, paths), F32), buffer((32, paths), F32),
            buffer((SIDE, paths), F32), buffer((SIDE, paths), F32),
            buffer((SIDE, SIDE), F32),
            buffer((2, terms, paths), BF16),
            buffer((2, seats, rows, 128), F32),
            buffer((seats, rows, 128), F32), buffer((seats, rows, 128), F32), buffer((seats, rows, 128), F32),
            buffer((2, seats, rows, 128), F32),
            buffer((1, terms), F32), buffer((path_devices, 1, terms), F32),
            buffer((1, terms), F32), buffer((path_devices, 1, terms), F32),
            buffer((2, terms, terms), F32), buffer((8, 8, 128), F32), buffer((8, 128), F32),
            buffer((2, scens, CHUNK, 128), F32),
            buffer((scens, CHUNK, 128), F32), buffer((scens, CHUNK, 128), F32), buffer((scens, CHUNK, 128), F32),
            buffer((CHUNK, 128), F32),
            buffer((seats, CHUNK // seats, 128), F32), buffer((seats, CHUNK // seats, 128), F32),
            buffer((seats, CHUNK // seats, 128), F32),
            buffer((2, scens, CHUNK, 128), F32),
            buffer((terms, 8), jnp.int32),
            pltpu.SMEM((8, 128), jnp.int32),
            buffer((4, 3, PAIRS, SIDE), BF16),
            buffer((own_rows, PAIRS, SIDE), BF16), buffer((own_rows, PAIRS, SIDE), BF16),
            buffer((own_rows, PAIRS, SIDE), BF16), buffer((own_rows, PAIRS, SIDE), BF16),
            buffer((own_rows, PAIRS, 256), BF16),
            buffer((256, proxy_terms), BF16), buffer((PAIRS, proxy_terms), F32),
            buffer((PAIRS, paths), F32), buffer((PAIRS, paths), F32),
            buffer((scens, tiles // scens, 1, 128), F32),
            buffer((path_devices, scens, 1, 128), F32),
            buffer((scens, 1, 128), F32), buffer((scens, 1, 128), F32),
            DMA, DMA,
            DMA((seats,)), DMA((seats,)), DMA((seats,)), DMA((seats,)), DMA((seats,)), DMA((seats,)),
            DMA((path_devices,)), DMA((path_devices,)), DMA((path_devices,)), DMA((path_devices,)),
            DMA, DMA,
            DMA((scens,)), DMA((scens,)), DMA((seats,)), DMA((seats,)), DMA((seats,)), DMA((seats,)),
            DMA((scens,)), DMA((scens,)), DMA((scens,)), DMA((scens,)),
            DMA((path_devices,)), DMA((path_devices,)),
            DMA((scens,)), DMA((scens,)), DMA,
        ],
        compiler_params=pltpu.CompilerParams(collective_id=0, has_side_effects=True),
        name="step",
    )(
        exercise_dates[0], discount[0], columns, states[0], itm_mask[0], surrender.transpose(1, 0, 2), terminal,
        ls_table.T, columns,
    )
    return (values, coefficients[None], proxy_gram, proxy_rhs[0, :own_rows])


def solution(mesh):
    placed = (
        P("scen", None, None, "path"),
        P("scen", None),
        P("scen", None, "path"),
        P("scen", None, "path"),
        P("scen", "path"),
        P("scen", None),
        P(),
        P(),
    )
    return jax.shard_map(
        on_device,
        mesh=mesh,
        in_specs=placed,
        out_specs=(
            P("scen", "path"),
            P("scen", None, None),
            P(("scen", "path"), None),
            P(("scen", "path")),
        ),
        check_vma=False,
    )
```

profile of v0, /device:TPU:1, one launch (start us, length us, event | category | flops | bytes accessed | tf_op | source)
XLA Modules:
  0.0 77.0 jit_solution(8093274072246337399)
XLA Ops:
  0.6 72.5 %step.1 = (f32[1,512]{1,0:T(1,128)}, f32[2,256]{1,0:T(2,128)}, f32[16,2048]{1,0:T(8,128)}, f32[1,128]{1,0:T(1,128)}) custom-call(s32[2]{0:T(128)} %bitcast.17, f32[2]{0:T(128)} %bitcast.18, s32[8,2048]{1,0:T(8,128)} %bitcast.11, f32[36,8,512]{2,1,0:T(8,128)} %bitcast.10, s32[2,512]{1,0:T(2,128)} %bitcast.15, f32[36,1,512]{2,1,0:T(1,128)} %bitcast.13, ...), custom_call_target="tpu_custom_call" | custom-call | tf_op jit(solution)/shard_map/step/pallas_call | solution.py:634
  73.1 0.0 copy-start.2
  73.1 0.0 copy-start.1
  73.1 0.6 copy-done.2
  73.7 0.5 slice_bitcast_fusion
  74.2 0.0 copy-done.1
  74.2 0.0 copy-start
  74.2 0.6 copy.15
  74.8 0.1 copy-done
  74.9 0.6 copy.16
  75.5 1.6 %copy.17 = f32[16,2048]{1,0:T(8,128)} copy(f32[16,2048]{1,0:T(8,128)} %get-tuple-element.18) | data formatting | bytes 262144
Async XLA Ops:
  73.1 0.6 copy-start.2
  73.1 1.1 %copy-start.1 = (f32[1,512]{1,0:T(1,128)S(1)}, f32[1,512]{1,0:T(1,128)}, u32[]{:S(2)}) copy-start(f32[1,512]{1,0:T(1,128)} %get-tuple-element.16) | copy-start | bytes 6148
  74.2 0.7 copy-start
where the time goes:
time: 77.2 us; the launch traced here: 77 us
  Pallas kernels  72.5 us (94%)
  local copies, waits for them, and re-layouts  3.9 us (5%)
    pallas_call x1, Pallas kernels, on_device(): pl.pallas_call(functools.partial(step_kernel, path_devices, scens), out_s...  72.5 us
    unnamed x9, local copies, waits for them, and re-layouts  3.39 us

commit v1 on v0

--- a/solution.py
+++ b/solution.py
@@ -211,8 +211,8 @@
     def rhs0_copy(q):
         return send(rhs0_own, rhs0_in.at[p], rhs0_s.at[q], rhs0_r.at[p], (s, q))
 
-    def half_copy():
-        return send(mom.at[1 - core], mom_half, half_s, half_r, partner)
+    def half_copy(t):
+        return send(mom.at[1 - core, t], mom_half.at[t], half_s.at[t], half_r.at[t], partner)
 
     def x_copy(t):
         return send(mom_acc.at[t], x_in.at[s], xr_s.at[t], xr_r.at[s], (t, p))
@@ -310,7 +310,10 @@
                 low_row - k * SIDE : top_row - k * SIDE, k * 128 : (k + 1) * 128
             ]
             low_row = top_row
-    half_copy().start()
+
+    @pl.loop(1, scens + 1)
+    def _(d):
+        half_copy(scen_peer(d)).start()
 
     @pl.loop(1, path_devices)
     def _(d):
@@ -331,13 +334,15 @@
 
     gram_forward(seat).start()
 
-    half_copy().wait()
-    for t in range(scens):
+    @pl.loop(1, scens)
+    def _(d):
+        t = scen_peer(d)
+        arrived(mom_half.at[t], half_r.at[t])
         mom_acc[t] = mom[core, t] + mom_half[t]
-
-    @pl.loop(1, scens)
-    def _(d):
-        x_copy(scen_peer(d)).start()
+        x_copy(t).start()
+
+    arrived(mom_half.at[s], half_r.at[s])
+    mom_acc[s] = mom[core, s] + mom_half[s]
 
     row = lax.broadcasted_iota(jnp.int32, high.shape, 0)
     for first, is_low in ((0, True), (4, False)):
@@ -358,19 +363,6 @@
         arrived(gram_all.at[core, j], ga_r.at[j])
         gram_forward(j).start()
 
-    @pl.loop(1, scens)
-    def _(d):
-        arrived(x_in.at[scen_peer(d)], xr_r.at[scen_peer(d)])
-
-    x_sum[...] = lax.fori_loop(1, scens, lambda d, carry: carry + x_in[scen_peer(d)], mom_acc[s])
-    own_part = CHUNK // seats
-    for j in range(seats):
-        seat_out[j] = x_sum[j * own_part : (j + 1) * own_part, :]
-
-    @pl.loop(1, seats)
-    def _(d):
-        seat_copy(seat_peer(d)).start()
-
     @pl.loop(0, seats)
     def _(j):
         arrived(gram_all.at[1 - core, j], gf_r.at[j])
@@ -388,6 +380,21 @@
     steps = terms // STEP
     eliminate(a_ref, e_ref, r_ref, 0, steps // 4)
 
+    @pl.loop(1, scens)
+    def _(d):
+        arrived(x_in.at[scen_peer(d)], xr_r.at[scen_peer(d)])
+
+    x_sum[...] = lax.fori_loop(1, scens, lambda d, carry: carry + x_in[scen_peer(d)], mom_acc[s])
+    own_part = CHUNK // seats
+    for j in range(seats):
+        seat_out[j] = x_sum[j * own_part : (j + 1) * own_part, :]
+
+    @pl.loop(1, seats)
+    def _(d):
+        seat_copy(seat_peer(d)).start()
+
+    eliminate(a_ref, e_ref, r_ref, steps // 4, steps // 2)
+
     @pl.loop(1, seats)
     def _(d):
         arrived(seat_in.at[seat_peer(d)], sr_r.at[seat_peer(d)])
@@ -400,7 +407,7 @@
     def _(d):
         seat_all_copy(seat_peer(d)).start()
 
-    eliminate(a_ref, e_ref, r_ref, steps // 4, steps // 2)
+    eliminate(a_ref, e_ref, r_ref, steps // 2, 3 * steps // 4)
 
     @pl.loop(1, seats)
     def _(d):
@@ -414,7 +421,7 @@
         full_copy(scen_peer(d)).start()
 
     forward_copy(s).start()
-    eliminate(a_ref, e_ref, r_ref, steps // 2, steps)
+    eliminate(a_ref, e_ref, r_ref, 3 * steps // 4, steps)
 
     @pl.loop(1, path_devices)
     def _(d):
@@ -458,6 +465,20 @@
         pattern[v, 1] = jnp.where(ones, 1.0, 0.0).astype(BF16)
         pattern[v, 2] = jnp.where(m == b + 2, 1.0, 0.0).astype(BF16)
 
+    own_tile.wait()
+
+    @pl.loop(0, rows)
+    def _(r):
+        def pattern_of(first):
+            result = None
+            for v in range(4):
+                block = pattern[v, mine[first + v, first_own + r]]
+                result = block if result is None else result * block
+            return result
+
+        pick_l[r] = pattern_of(0)
+        pick_r[r] = pattern_of(4)
+
     @pl.loop(1, scens)
     def _(d):
         t = scen_peer(d)
@@ -495,20 +516,6 @@
     @pl.loop(1, path_devices)
     def _(d):
         part_copy(path_peer(d)).start()
-
-    own_tile.wait()
-
-    @pl.loop(0, rows)
-    def _(r):
-        def pattern_of(first):
-            result = None
-            for v in range(4):
-                block = pattern[v, mine[first + v, first_own + r]]
-                result = block if result is None else result * block
-            return result
-
-        pick_l[r] = pattern_of(0)
-        pick_r[r] = pattern_of(4)
 
     @pl.loop(0, scens)
     def _(t):
@@ -529,37 +536,28 @@
     y_high[...] = yh.reshape(y_high.shape)
     y_low[...] = yl.reshape(y_low.shape)
 
-    @pl.loop(1, path_devices)
-    def _(d):
-        arrived(parts_in.at[path_peer(d)], pa_r.at[path_peer(d)])
-
-    def add_part(d, carry):
-        return carry + parts_in[path_peer(d)]
-
-    mine_part[...] = lax.fori_loop(1, path_devices, add_part, parts[:, p // 8])
-
-    @pl.loop(1, scens)
-    def _(d):
-        mine_copy(scen_peer(d)).start()
-
-    z_pack[...] = jnp.zeros(z_pack.shape, BF16)
-
-    @pl.loop(0, rows)
-    def _(r):
+    def second_product(r):
         zh, zl = halves(nt(pick_r[r], y_high[r]) + nt(pick_r[r], y_low[r]))
         z_pack[r, :, 0:PAIRS] = zh
         z_pack[r, :, 128 : 128 + PAIRS] = zl
 
+    z_pack[...] = jnp.zeros(z_pack.shape, BF16)
+    pl.loop(0, rows // 2)(second_product)
+
+    @pl.loop(1, path_devices)
+    def _(d):
+        arrived(parts_in.at[path_peer(d)], pa_r.at[path_peer(d)])
+
+    def add_part(d, carry):
+        return carry + parts_in[path_peer(d)]
+
+    mine_part[...] = lax.fori_loop(1, path_devices, add_part, parts[:, p // 8])
+
     @pl.loop(1, scens)
     def _(d):
-        arrived(mine_in.at[scen_peer(d)], pb_r.at[scen_peer(d)])
-
-    def add_mine(d, carry):
-        return carry + mine_in[scen_peer(d)]
-
-    last = lax.fori_loop(1, scens, add_mine, mine_part[s])
-    last = pltpu.roll(jnp.broadcast_to(last, (8, 128)), (128 - rows * (p % 8)) % 128, 1)
-    rhs_out[...] = last[0:1] * own_scale
+        mine_copy(scen_peer(d)).start()
+
+    pl.loop(rows // 2, rows)(second_product)
 
     column = None
     for v in range(8):
@@ -578,6 +576,17 @@
             lines.append(jnp.sum(picked, axis=0, keepdims=True) * (column * own))
         gram_out[pl.ds(pl.multiple_of(block * 8, 8), 8), :] = jnp.concatenate(lines, axis=0)
 
+    @pl.loop(1, scens)
+    def _(d):
+        arrived(mine_in.at[scen_peer(d)], pb_r.at[scen_peer(d)])
+
+    def add_mine(d, carry):
+        return carry + mine_in[scen_peer(d)]
+
+    last = lax.fori_loop(1, scens, add_mine, mine_part[s])
+    last = pltpu.roll(jnp.broadcast_to(last, (8, 128)), (128 - rows * (p % 8)) % 128, 1)
+    rhs_out[...] = last[0:1] * own_scale
+
     gram_forward(seat).wait_send()
 
     @pl.loop(1, seats)
@@ -609,7 +618,15 @@
 
     @pl.loop(0, scens)
     def _(t):
+        half_copy(t).wait_send()
         forward_copy(t).wait_send()
+
+
+def finish_kernel(values, coef, gram, rhs, values_out, coef_out, gram_out, rhs_out):
+    values_out[...] = values[...]
+    coef_out[...] = coef[...]
+    gram_out[...] = gram[...]
+    rhs_out[...] = rhs[:, 0 : rhs_out.shape[1]]
 
 
 VMEM = pl.BlockSpec(memory_space=pltpu.VMEM)
@@ -672,7 +689,7 @@
             DMA, DMA,
             DMA((seats,)), DMA((seats,)), DMA((seats,)), DMA((seats,)), DMA((seats,)), DMA((seats,)),
             DMA((path_devices,)), DMA((path_devices,)), DMA((path_devices,)), DMA((path_devices,)),
-            DMA, DMA,
+            DMA((scens,)), DMA((scens,)),
             DMA((scens,)), DMA((scens,)), DMA((seats,)), DMA((seats,)), DMA((seats,)), DMA((seats,)),
             DMA((scens,)), DMA((scens,)), DMA((scens,)), DMA((scens,)),
             DMA((path_devices,)), DMA((path_devices,)),
@@ -684,7 +701,19 @@
         exercise_dates[0], discount[0], columns, states[0], itm_mask[0], surrender.transpose(1, 0, 2), terminal,
         ls_table.T, columns,
     )
-    return (values, coefficients[None], proxy_gram, proxy_rhs[0, :own_rows])
+    values, coefficients, proxy_gram, proxy_rhs = pl.pallas_call(
+        finish_kernel,
+        out_shape=(
+            jax.ShapeDtypeStruct((1, paths), F32),
+            jax.ShapeDtypeStruct((2, terms), F32),
+            jax.ShapeDtypeStruct((own_rows, proxy_terms), F32),
+            jax.ShapeDtypeStruct((1, own_rows), F32),
+        ),
+        in_specs=[VMEM] * 4,
+        out_specs=[VMEM] * 4,
+        name="finish",
+    )(values, coefficients, proxy_gram, proxy_rhs)
+    return (values, coefficients[None], proxy_gram, proxy_rhs[0])
 
 
 def solution(mesh):

time: 77.2 us -> 69.8 us (0.904)
  local copies, waits for them, and re-layouts: 3.9 us -> 0 us
  Pallas kernels: 72.5 us -> 69 us
    pallas_call x1, Pallas kernels: 72.5 us -> 67.4 us  [on_device(): pl.pallas_call(functools.partial(step_kernel, path_devices, scens), out_s...]
    unnamed x9 -> x0, local copies, waits for them, and re-layouts: 3.39 us -> none
    pallas_call x0 -> x1, Pallas kernels: none -> 1.59 us  [on_device(): pl.pallas_call(finish_kernel, out_shape=(jax.ShapeDtypeStruct((1, paths),...]
where the time goes in v1:
time: 69.8 us; the launch traced here: 69.7 us
  Pallas kernels  69 us (99%)
    pallas_call x1, Pallas kernels, on_device(): pl.pallas_call(functools.partial(step_kernel, path_devices, scens), out_s...  67.4 us
    pallas_call x1, Pallas kernels, on_device(): pl.pallas_call(finish_kernel, out_shape=(jax.ShapeDtypeStruct((1, paths),...  1.59 us

profile of v1, /device:TPU:1, one launch (start us, length us, event | category | flops | bytes accessed | tf_op | source)
XLA Modules:
  0.0 69.7 jit_solution(7213387089912658413)
XLA Ops:
  0.6 67.4 %step.1 = (f32[1,512]{1,0:T(1,128)}, f32[2,256]{1,0:T(2,128)}, f32[16,2048]{1,0:T(8,128)}, f32[1,128]{1,0:T(1,128)}) custom-call(s32[2]{0:T(128)} %bitcast.15, f32[2]{0:T(128)} %bitcast.16, s32[8,2048]{1,0:T(8,128)} %bitcast.10, f32[36,8,512]{2,1,0:T(8,128)} %bitcast.9, s32[2,512]{1,0:T(2,128)} %bitcast.14, f32[36,1,512]{2,1,0:T(1,128)} %bitcast.12, ...), custom_call_target="tpu_custom_call" | custom-call | tf_op jit(solution)/shard_map/step/pallas_call | solution.py:651
  68.1 1.6 %finish.1 = (f32[1,512]{1,0:T(1,128)}, f32[2,256]{1,0:T(2,128)}, f32[16,2048]{1,0:T(8,128)}, f32[1,16]{1,0:T(1,128)}) custom-call(f32[1,512]{1,0:T(1,128)} %get-tuple-element.12.values, f32[2,256]{1,0:T(2,128)} %get-tuple-element.13.coef, f32[16,2048]{1,0:T(8,128)} %get-tuple-element.14.gram, f32[1,128]{1,0:T(1,128)} %get-tuple-element.15.rhs), custom_call_target="tpu_custom_call" | custom-call | tf_op jit(solution)/shard_map/finish/pallas_call | solution.py:704

commit v2 on v1

--- a/solution.py
+++ b/solution.py
@@ -195,21 +195,20 @@
         return send(gram.at[1 - core], gram_half, gh_s, gh_r, partner)
 
     def gram_copy(j):
-        return send(gram_acc.at[j], gram_in.at[seat], g_s.at[j], g_r.at[seat], seat_id(j))
+        return send(gram_acc.at[j], gram_in.at[seat], g_s, g_r, seat_id(j))
 
     def gram_all_copy(j):
         block = gram_all.at[core, seat]
-        return send(block, block, ga_s.at[j], ga_r.at[seat], seat_id(j))
-
-    def gram_forward(j):
-        block = gram_all.at[core, j]
-        return send(block, block, gf_s.at[j], gf_r.at[j], partner)
+        return send(block, block, ga_s, ga_r, seat_id(j))
+
+    def gram_forward():
+        return send(gram_all.at[core], gram_all.at[core], gf_s, gf_r, partner)
 
     def rhs_copy(q):
-        return send(rhs_own, rhs_in.at[p], rhs_s.at[q], rhs_r.at[p], (s, q))
+        return send(rhs_own, rhs_in.at[p], rhs_s, rhs_r, (s, q))
 
     def rhs0_copy(q):
-        return send(rhs0_own, rhs0_in.at[p], rhs0_s.at[q], rhs0_r.at[p], (s, q))
+        return send(rhs0_own, rhs0_in.at[p], rhs0_s, rhs0_r, (s, q))
 
     def half_copy(t):
         return send(mom.at[1 - core, t], mom_half.at[t], half_s.at[t], half_r.at[t], partner)
@@ -233,7 +232,7 @@
         return send(block, block, fw_s.at[t], fw_r.at[t], partner)
 
     def part_copy(q):
-        return send(parts.at[:, q // 8], parts_in.at[p], pa_s.at[q], pa_r.at[p], (s, q))
+        return send(parts.at[:, q // 8], parts_in.at[p], pa_s, pa_r, (s, q))
 
     def mine_copy(t):
         return send(mine_part.at[t], mine_in.at[s], pb_s.at[t], pb_r.at[s], (t, p))
@@ -319,9 +318,7 @@
     def _(d):
         rhs_copy(path_peer(d)).start()
 
-    @pl.loop(1, seats)
-    def _(d):
-        arrived(gram_in.at[seat_peer(d)], g_r.at[seat_peer(d)])
+    arrived(gram_in.at[pl.ds(0, seats - 1)], g_r)
 
     def add_gram(d, carry):
         return carry + gram_in[seat_peer(d)]
@@ -332,7 +329,6 @@
     def _(d):
         gram_all_copy(seat_peer(d)).start()
 
-    gram_forward(seat).start()
 
     @pl.loop(1, scens)
     def _(d):
@@ -357,15 +353,10 @@
         else:
             high[...] = hot
 
-    @pl.loop(1, seats)
-    def _(d):
-        j = seat_peer(d)
-        arrived(gram_all.at[core, j], ga_r.at[j])
-        gram_forward(j).start()
-
-    @pl.loop(0, seats)
-    def _(j):
-        arrived(gram_all.at[1 - core, j], gf_r.at[j])
+    arrived(gram_all.at[core, pl.ds(0, seats - 1)], ga_r)
+    gram_forward().start()
+
+    arrived(gram_all.at[1 - core], gf_r)
 
     ri = lax.broadcasted_iota(jnp.int32, (128, 128), 0)
     ci = lax.broadcasted_iota(jnp.int32, (128, 128), 1)
@@ -423,9 +414,7 @@
     forward_copy(s).start()
     eliminate(a_ref, e_ref, r_ref, 3 * steps // 4, steps)
 
-    @pl.loop(1, path_devices)
-    def _(d):
-        arrived(rhs_in.at[path_peer(d)], rhs_r.at[path_peer(d)])
+    arrived(rhs_in.at[pl.ds(0, path_devices - 1)], rhs_r)
 
     def add_rhs(d, carry):
         return carry + rhs_in[path_peer(d)]
@@ -479,15 +468,33 @@
         pick_l[r] = pattern_of(0)
         pick_r[r] = pattern_of(4)
 
+    arrived(gram_in.at[pl.ds(0, seats - 1)], g_s)
+    arrived(gram_in.at[pl.ds(0, seats - 1)], ga_s)
+    arrived(gram_all.at[core], gf_s)
+    arrived(rhs_in.at[pl.ds(0, path_devices - 1)], rhs_s)
+
+    @pl.loop(1, seats)
+    def _(d):
+        j = seat_peer(d)
+        seat_copy(j).wait_send()
+        seat_all_copy(j).wait_send()
+
+    @pl.loop(1, scens)
+    def _(d):
+        x_copy(scen_peer(d)).wait_send()
+
+    @pl.loop(0, scens)
+    def _(t):
+        half_copy(t).wait_send()
+
     @pl.loop(1, scens)
     def _(d):
         t = scen_peer(d)
         arrived(full.at[core, t], xa_r.at[t])
         forward_copy(t).start()
 
-    @pl.loop(1, path_devices)
-    def _(d):
-        arrived(rhs0_in.at[path_peer(d)], rhs0_r.at[path_peer(d)])
+    arrived(rhs0_in.at[pl.ds(0, path_devices - 1)], rhs0_r)
+    arrived(rhs0_in.at[pl.ds(0, path_devices - 1)], rhs0_s)
 
     def add_rhs0(d, carry):
         return carry + rhs0_in[path_peer(d)]
@@ -544,9 +551,7 @@
     z_pack[...] = jnp.zeros(z_pack.shape, BF16)
     pl.loop(0, rows // 2)(second_product)
 
-    @pl.loop(1, path_devices)
-    def _(d):
-        arrived(parts_in.at[path_peer(d)], pa_r.at[path_peer(d)])
+    arrived(parts_in.at[pl.ds(0, path_devices - 1)], pa_r)
 
     def add_part(d, carry):
         return carry + parts_in[path_peer(d)]
@@ -587,38 +592,16 @@
     last = pltpu.roll(jnp.broadcast_to(last, (8, 128)), (128 - rows * (p % 8)) % 128, 1)
     rhs_out[...] = last[0:1] * own_scale
 
-    gram_forward(seat).wait_send()
-
-    @pl.loop(1, seats)
-    def _(d):
-        j = seat_peer(d)
-        gram_copy(j).wait_send()
-        gram_all_copy(j).wait_send()
-        gram_forward(j).wait_send()
-
-    @pl.loop(1, path_devices)
-    def _(d):
-        q = path_peer(d)
-        rhs_copy(q).wait_send()
-        rhs0_copy(q).wait_send()
-        part_copy(q).wait_send()
-
-    @pl.loop(1, seats)
-    def _(d):
-        j = seat_peer(d)
-        seat_copy(j).wait_send()
-        seat_all_copy(j).wait_send()
+    arrived(parts_in.at[pl.ds(0, path_devices - 1)], pa_s)
 
     @pl.loop(1, scens)
     def _(d):
         t = scen_peer(d)
-        x_copy(t).wait_send()
         full_copy(t).wait_send()
         mine_copy(t).wait_send()
 
     @pl.loop(0, scens)
     def _(t):
-        half_copy(t).wait_send()
         forward_copy(t).wait_send()
 
 
@@ -687,12 +670,12 @@
             buffer((path_devices, scens, 1, 128), F32),
             buffer((scens, 1, 128), F32), buffer((scens, 1, 128), F32),
             DMA, DMA,
-            DMA((seats,)), DMA((seats,)), DMA((seats,)), DMA((seats,)), DMA((seats,)), DMA((seats,)),
-            DMA((path_devices,)), DMA((path_devices,)), DMA((path_devices,)), DMA((path_devices,)),
+            DMA, DMA, DMA, DMA, DMA, DMA,
+            DMA, DMA, DMA, DMA,
             DMA((scens,)), DMA((scens,)),
             DMA((scens,)), DMA((scens,)), DMA((seats,)), DMA((seats,)), DMA((seats,)), DMA((seats,)),
             DMA((scens,)), DMA((scens,)), DMA((scens,)), DMA((scens,)),
-            DMA((path_devices,)), DMA((path_devices,)),
+            DMA, DMA,
             DMA((scens,)), DMA((scens,)), DMA,
         ],
         compiler_params=pltpu.CompilerParams(collective_id=0, has_side_effects=True),

time: 69.8 us -> 66 us (0.946)
  Pallas kernels: 69 us -> 65.2 us
    pallas_call x1, Pallas kernels: 67.4 us -> 63.6 us  [on_device(): pl.pallas_call(functools.partial(step_kernel, path_devices, scens), out_s...]
where the time goes in v2:
time: 66 us; the launch traced here: 65.8 us
  Pallas kernels  65.2 us (99%)
    pallas_call x1, Pallas kernels, on_device(): pl.pallas_call(functools.partial(step_kernel, path_devices, scens), out_s...  63.6 us
    pallas_call x1, Pallas kernels, on_device(): pl.pallas_call(finish_kernel, out_shape=(jax.ShapeDtypeStruct((1, paths),...  1.59 us

profile of v2, /device:TPU:1, one launch (start us, length us, event | category | flops | bytes accessed | tf_op | source)
XLA Modules:
  0.0 65.8 jit_solution(3506586987375449931)
XLA Ops:
  0.6 63.6 %step.1 = (f32[1,512]{1,0:T(1,128)}, f32[2,256]{1,0:T(2,128)}, f32[16,2048]{1,0:T(8,128)}, f32[1,128]{1,0:T(1,128)}) custom-call(s32[2]{0:T(128)} %bitcast.15, f32[2]{0:T(128)} %bitcast.16, s32[8,2048]{1,0:T(8,128)} %bitcast.10, f32[36,8,512]{2,1,0:T(8,128)} %bitcast.9, s32[2,512]{1,0:T(2,128)} %bitcast.14, f32[36,1,512]{2,1,0:T(1,128)} %bitcast.12, ...), custom_call_target="tpu_custom_call" | custom-call | tf_op jit(solution)/shard_map/step/pallas_call | solution.py:634
  64.2 1.6 %finish.1 = (f32[1,512]{1,0:T(1,128)}, f32[2,256]{1,0:T(2,128)}, f32[16,2048]{1,0:T(8,128)}, f32[1,16]{1,0:T(1,128)}) custom-call(f32[1,512]{1,0:T(1,128)} %get-tuple-element.12.values, f32[2,256]{1,0:T(2,128)} %get-tuple-element.13.coef, f32[16,2048]{1,0:T(8,128)} %get-tuple-element.14.gram, f32[1,128]{1,0:T(1,128)} %get-tuple-element.15.rhs), custom_call_target="tpu_custom_call" | custom-call | tf_op jit(solution)/shard_map/finish/pallas_call | solution.py:687

commit v3 on v2

--- a/solution.py
+++ b/solution.py
@@ -122,6 +122,28 @@
     return a
 
 
+def thirds(x):
+    high = x.astype(BF16).astype(F32)
+    rest = x - high
+    mid = rest.astype(BF16).astype(F32)
+    return high, mid, rest - mid
+
+
+def pack_left(x):
+    a, b, c = thirds(x)
+    lane = lax.broadcasted_iota(jnp.int32, x.shape, 1)
+    first = jnp.where(lane < 64, jnp.where(lane < 32, a, pltpu.roll(a, 32, 1)),
+                      jnp.where(lane < 96, pltpu.roll(b, 64, 1), pltpu.roll(b, 96, 1)))
+    second = jnp.where(lane < 32, a, jnp.where(lane < 64, pltpu.roll(c, 32, 1), 0.0))
+    return jnp.concatenate([first, second], axis=1).astype(BF16)
+
+
+def pack_right(x):
+    a, b, c = thirds(x)
+    zero = jnp.zeros_like(a)
+    return jnp.concatenate([a, b, a, b, c, a, zero, zero], axis=0).astype(BF16)
+
+
 def eliminate(a_ref, e_ref, r_ref, start, stop):
     n = a_ref.shape[1]
     lane = lax.broadcasted_iota(jnp.int32, (STEP, n), 1)
@@ -130,15 +152,14 @@
 
     def body(k, _):
         first = [a_ref[d, 0:STEP, 0:128] for d in range(2)]
+        lefts = [pack_left(a_ref[d, STEP:, 0:128]) for d in range(2)]
+        rights = [pack_right(a_ref[d, 0:STEP, :]) for d in range(2)]
         both = leaf(jnp.where(lane1 < 64, first[0], pltpu.roll(first[1], 64, 1)), e_ref, r_ref)
         for d, neg in enumerate((both, pltpu.roll(both, 64, 1))):
-            r = a_ref[d, 0:STEP, :]
             rest = a_ref[d, STEP:, :]
-            x = jnp.dot(neg[:, 0:STEP], r, precision=HI, preferred_element_type=F32)
+            x = nn(pack_left(neg), rights[d])
             xt = jnp.where(lane < STEP, jnp.concatenate([neg, neg], axis=1), -x)
-            new = jnp.where(lane2 < STEP, 0.0, rest) - jnp.dot(
-                rest[:, 0:STEP], xt, precision=HI, preferred_element_type=F32
-            )
+            new = jnp.where(lane2 < STEP, 0.0, rest) - nn(lefts[d], pack_right(xt))
             a_ref[d, 0 : n - STEP, :] = pltpu.roll(new, n - STEP, 1)
             a_ref[d, n - STEP :, :] = pltpu.roll(xt, n - STEP, 1)
         return 0
@@ -217,11 +238,11 @@
         return send(mom_acc.at[t], x_in.at[s], xr_s.at[t], xr_r.at[s], (t, p))
 
     def seat_copy(j):
-        return send(seat_out.at[j], seat_in.at[seat], sr_s.at[j], sr_r.at[seat], seat_id(j))
+        return send(seat_out.at[j], seat_in.at[seat], sr_s, sr_r, seat_id(j))
 
     def seat_all_copy(j):
         block = seat_all.at[seat]
-        return send(block, block, sa_s.at[j], sa_r.at[seat], seat_id(j))
+        return send(block, block, sa_s, sa_r, seat_id(j))
 
     def full_copy(t):
         block = full.at[core, s]
@@ -254,19 +275,25 @@
     ls_table[...] = ls_columns[...].T
 
     early = states[dates[0]]
+    level_one = (early, states[dates[1]])
+    level_two = [(u * u - 1.0) * ROOT_HALF for u in level_one]
+    for top in range(0, terms, 32):
+        t = ls_table[top : top + 32, :]
+        result = [None, None]
+        for v in range(8):
+            degree = jnp.broadcast_to(t[:, v : v + 1], (32, 128))
+            is_one = jnp.concatenate([degree == 1] * (paths // 128), axis=1)
+            is_two = jnp.concatenate([degree == 2] * (paths // 128), axis=1)
+            for d in range(2):
+                level = jnp.where(
+                    is_one,
+                    level_one[d][v : v + 1, :],
+                    jnp.where(is_two, level_two[d][v : v + 1, :], 1.0),
+                )
+                result[d] = level if v == 0 else result[d] * level
+        for d in range(2):
+            design[d, top : top + 32, :] = result[d].astype(BF16)
     for backward in (1, 0):
-        u = early if backward == 0 else states[dates[1]]
-        h = (u * u - 1.0) * ROOT_HALF
-        for top in range(0, terms, 32):
-            t = ls_table[top : top + 32, :]
-            result = None
-            for v in range(8):
-                degree = jnp.broadcast_to(t[:, v : v + 1], (32, paths))
-                level = jnp.where(
-                    degree == 1, u[v : v + 1, :], jnp.where(degree == 2, h[v : v + 1, :], 1.0)
-                )
-                result = level if result is None else result * level
-            design[backward, top : top + 32, :] = result.astype(BF16)
         live = design[backward]
         weighted = live * mask[backward : backward + 1, :].astype(F32).astype(BF16)
         g = nt(weighted, live)
@@ -386,9 +413,7 @@
 
     eliminate(a_ref, e_ref, r_ref, steps // 4, steps // 2)
 
-    @pl.loop(1, seats)
-    def _(d):
-        arrived(seat_in.at[seat_peer(d)], sr_r.at[seat_peer(d)])
+    arrived(seat_in.at[pl.ds(0, seats - 1)], sr_r)
 
     seat_all[seat] = lax.fori_loop(
         1, seats, lambda d, carry: carry + seat_in[seat_peer(d)], seat_out[seat]
@@ -400,9 +425,7 @@
 
     eliminate(a_ref, e_ref, r_ref, steps // 2, 3 * steps // 4)
 
-    @pl.loop(1, seats)
-    def _(d):
-        arrived(seat_all.at[seat_peer(d)], sa_r.at[seat_peer(d)])
+    arrived(seat_all.at[pl.ds(0, seats - 1)], sa_r)
 
     for j in range(seats):
         full[core, s, j * own_part : (j + 1) * own_part, :] = seat_all[j]
@@ -473,11 +496,8 @@
     arrived(gram_all.at[core], gf_s)
     arrived(rhs_in.at[pl.ds(0, path_devices - 1)], rhs_s)
 
-    @pl.loop(1, seats)
-    def _(d):
-        j = seat_peer(d)
-        seat_copy(j).wait_send()
-        seat_all_copy(j).wait_send()
+    arrived(seat_in.at[pl.ds(0, seats - 1)], sr_s)
+    arrived(seat_in.at[pl.ds(0, seats - 1)], sa_s)
 
     @pl.loop(1, scens)
     def _(d):
@@ -673,7 +693,7 @@
             DMA, DMA, DMA, DMA, DMA, DMA,
             DMA, DMA, DMA, DMA,
             DMA((scens,)), DMA((scens,)),
-            DMA((scens,)), DMA((scens,)), DMA((seats,)), DMA((seats,)), DMA((seats,)), DMA((seats,)),
+            DMA((scens,)), DMA((scens,)), DMA, DMA, DMA, DMA,
             DMA((scens,)), DMA((scens,)), DMA((scens,)), DMA((scens,)),
             DMA, DMA,
             DMA((scens,)), DMA((scens,)), DMA,

time: 66 us -> 64.8 us (0.982)
  Pallas kernels: 65.2 us -> 64 us
    pallas_call x1, Pallas kernels: 63.6 us -> 62.4 us  [on_device(): pl.pallas_call(functools.partial(step_kernel, path_devices, scens), out_s...]
where the time goes in v3:
time: 64.8 us; the launch traced here: 64.7 us
  Pallas kernels  64 us (99%)
    pallas_call x1, Pallas kernels, on_device(): pl.pallas_call(functools.partial(step_kernel, path_devices, scens), out_s...  62.4 us
    pallas_call x1, Pallas kernels, on_device(): pl.pallas_call(finish_kernel, out_shape=(jax.ShapeDtypeStruct((1, paths),...  1.59 us

profile of v3, /device:TPU:1, one launch (start us, length us, event | category | flops | bytes accessed | tf_op | source)
XLA Modules:
  0.0 64.7 jit_solution(17474729303921387786)
XLA Ops:
  0.6 62.4 %step.1 = (f32[1,512]{1,0:T(1,128)}, f32[2,256]{1,0:T(2,128)}, f32[16,2048]{1,0:T(8,128)}, f32[1,128]{1,0:T(1,128)}) custom-call(s32[2]{0:T(128)} %bitcast.15, f32[2]{0:T(128)} %bitcast.16, s32[8,2048]{1,0:T(8,128)} %bitcast.10, f32[36,8,512]{2,1,0:T(8,128)} %bitcast.9, s32[2,512]{1,0:T(2,128)} %bitcast.14, f32[36,1,512]{2,1,0:T(1,128)} %bitcast.12, ...), custom_call_target="tpu_custom_call" | custom-call | tf_op jit(solution)/shard_map/step/pallas_call | solution.py:654
  63.1 1.6 %finish.1 = (f32[1,512]{1,0:T(1,128)}, f32[2,256]{1,0:T(2,128)}, f32[16,2048]{1,0:T(8,128)}, f32[1,16]{1,0:T(1,128)}) custom-call(f32[1,512]{1,0:T(1,128)} %get-tuple-element.12.values, f32[2,256]{1,0:T(2,128)} %get-tuple-element.13.coef, f32[16,2048]{1,0:T(8,128)} %get-tuple-element.14.gram, f32[1,128]{1,0:T(1,128)} %get-tuple-element.15.rhs), custom_call_target="tpu_custom_call" | custom-call | tf_op jit(solution)/shard_map/finish/pallas_call | solution.py:707

commit v4 on v3

--- a/solution.py
+++ b/solution.py
@@ -396,7 +396,7 @@
         a_ref[d, 0:128, 128:256] = corner.T
         a_ref[d, 128:256, 128:256] = stack[256:384, :] + ridge
     steps = terms // STEP
-    eliminate(a_ref, e_ref, r_ref, 0, steps // 4)
+    eliminate(a_ref, e_ref, r_ref, 0, 1)
 
     @pl.loop(1, scens)
     def _(d):
@@ -411,7 +411,7 @@
     def _(d):
         seat_copy(seat_peer(d)).start()
 
-    eliminate(a_ref, e_ref, r_ref, steps // 4, steps // 2)
+    eliminate(a_ref, e_ref, r_ref, 1, 3)
 
     arrived(seat_in.at[pl.ds(0, seats - 1)], sr_r)
 
@@ -423,7 +423,7 @@
     def _(d):
         seat_all_copy(seat_peer(d)).start()
 
-    eliminate(a_ref, e_ref, r_ref, steps // 2, 3 * steps // 4)
+    eliminate(a_ref, e_ref, r_ref, 3, 5)
 
     arrived(seat_all.at[pl.ds(0, seats - 1)], sa_r)
 
@@ -435,7 +435,7 @@
         full_copy(scen_peer(d)).start()
 
     forward_copy(s).start()
-    eliminate(a_ref, e_ref, r_ref, 3 * steps // 4, steps)
+    eliminate(a_ref, e_ref, r_ref, 5, 8)
 
     arrived(rhs_in.at[pl.ds(0, path_devices - 1)], rhs_r)
 

time: 64.8 us -> 66.4 us (1.025)
  Pallas kernels: 64 us -> 65.6 us
    pallas_call x1, Pallas kernels: 62.4 us -> 64 us  [on_device(): pl.pallas_call(functools.partial(step_kernel, path_devices, scens), out_s...]
where the time goes in v4:
time: 66.4 us; the launch traced here: 66.3 us
  Pallas kernels  65.6 us (99%)
    pallas_call x1, Pallas kernels, on_device(): pl.pallas_call(functools.partial(step_kernel, path_devices, scens), out_s...  64 us
    pallas_call x1, Pallas kernels, on_device(): pl.pallas_call(finish_kernel, out_shape=(jax.ShapeDtypeStruct((1, paths),...  1.59 us

profile of v4, /device:TPU:1, one launch (start us, length us, event | category | flops | bytes accessed | tf_op | source)
XLA Modules:
  0.0 66.3 jit_solution(16900165741182175545)
XLA Ops:
  0.6 64.0 %step.1 = (f32[1,512]{1,0:T(1,128)}, f32[2,256]{1,0:T(2,128)}, f32[16,2048]{1,0:T(8,128)}, f32[1,128]{1,0:T(1,128)}) custom-call(s32[2]{0:T(128)} %bitcast.15, f32[2]{0:T(128)} %bitcast.16, s32[8,2048]{1,0:T(8,128)} %bitcast.10, f32[36,8,512]{2,1,0:T(8,128)} %bitcast.9, s32[2,512]{1,0:T(2,128)} %bitcast.14, f32[36,1,512]{2,1,0:T(1,128)} %bitcast.12, ...), custom_call_target="tpu_custom_call" | custom-call | tf_op jit(solution)/shard_map/step/pallas_call | solution.py:654
  64.7 1.6 %finish.1 = (f32[1,512]{1,0:T(1,128)}, f32[2,256]{1,0:T(2,128)}, f32[16,2048]{1,0:T(8,128)}, f32[1,16]{1,0:T(1,128)}) custom-call(f32[1,512]{1,0:T(1,128)} %get-tuple-element.12.values, f32[2,256]{1,0:T(2,128)} %get-tuple-element.13.coef, f32[16,2048]{1,0:T(8,128)} %get-tuple-element.14.gram, f32[1,128]{1,0:T(1,128)} %get-tuple-element.15.rhs), custom_call_target="tpu_custom_call" | custom-call | tf_op jit(solution)/shard_map/finish/pallas_call | solution.py:707
